TPU v7x, 32 devices: a whole 2x2x4 slice. The times are simulated.
32 devices in a mesh: grp: 2 (over x), wide: 16 (over z, y, core).
Axes of the slice: x: 2, y: 2, z: 4, core: 2. Of those that a mesh axis runs over, the one named last changes fastest.
Arguments:
- raw: bfloat16 [4096, 16, 2048], P(('grp', 'wide')), parts along dimension 0, may hold values from -6 to 6
- cell_feed: int32 [1024], replicated, may hold values from 0 to 1023, each once
- dm_delay: int32 [1024, 1024], replicated, may hold values from 0 to 15
Outputs:
- dedispersed: float32 [2048, 16, 1024], P(('grp', 'wide')), parts along dimension 0
There are 2 independent parts, one for each index of `grp`. A program takes and returns all parts, laid end to end along the dimension named above; an argument that names none is the same for every part. Nothing has to cross between parts.
Inputs may be any that keep to these rules, and one draw needn't show every extreme that they name: `cell_feed`: every antenna stands at exactly one cell.
All inputs are finite; a program needn't handle non-finite values.
Results may differ from a plain program's by a relative error of at most 0.0084.
Values may be sent and summed in bfloat16 or wider, within the bound.
No kernel may reach another device: no remote copies, remote signals or barrier semaphores. Data moves between devices by JAX's collectives and lax.ppermute only.
A program may use at most 128 MiB of HBM per device.

v0:
```python
import math
import jax
import jax.numpy as jnp
import numpy as np
from jax import lax
from jax.sharding import PartitionSpec as P

EAST_COSINE = np.array([[1, 1, 1, 1], [1, 0, -1, 0], [1, -1, 1, -1], [1, 0, -1, 0]], np.float32)
EAST_SINE = np.array([[0, 0, 0, 0], [0, 1, 0, -1], [0, 0, 0, 0], [0, -1, 0, 1]], np.float32)


def phase_pair(count, length):
    angle = (count % length).astype(jnp.float32) * (2.0 * math.pi / length)
    return (jnp.cos(angle), jnp.sin(angle))


def channel_table(samples, width):
    sample_ids = lax.broadcasted_iota(jnp.int32, (samples, width), 0)
    freq_ids = lax.broadcasted_iota(jnp.int32, (samples, width), 1)
    cosine, sine = phase_pair(sample_ids * freq_ids, samples)
    factor = 1.0 / math.sqrt(samples)
    return jnp.concatenate([cosine * factor, -sine * factor], axis=1).astype(jnp.bfloat16)


def sky_table(cells):
    rows = lax.broadcasted_iota(jnp.int32, (cells, cells), 0)
    cols = lax.broadcasted_iota(jnp.int32, (cells, cells), 1)
    cosine, sine = phase_pair(rows * cols, cells)
    real_row = jnp.stack([cosine, sine], axis=-1)
    imag_row = jnp.stack([-sine, cosine], axis=-1)
    factor = 1.0 / math.sqrt(cells)
    return (jnp.stack([real_row, imag_row], axis=1) * factor).astype(jnp.bfloat16)


def transform_table(frames):
    terms = frames // 2 + 1
    harmonic = lax.broadcasted_iota(jnp.int32, (terms, frames), 0)
    moment = lax.broadcasted_iota(jnp.int32, (terms, frames), 1)
    cosine, sine = phase_pair(harmonic * moment, frames)
    return jnp.stack([cosine, -sine]).astype(jnp.bfloat16)


def beam_power(spec, feed_index, table):
    grid = jnp.take(spec, feed_index.reshape(-1), axis=0)
    grid = grid.reshape(feed_index.shape + spec.shape[1:])
    beams = jnp.einsum("joni,penrif->poerfj", table, grid, preferred_element_type=jnp.float32)
    real_part = beams[:, 0]
    imag_part = beams[:, 1]
    cosines = jnp.asarray(EAST_COSINE)
    sines = jnp.asarray(EAST_SINE)
    high = lax.Precision.HIGHEST
    east_real = 0.5 * (
        jnp.einsum("qe,perfj->prfqj", cosines, real_part, precision=high)
        + jnp.einsum("qe,perfj->prfqj", sines, imag_part, precision=high)
    )
    east_imag = 0.5 * (
        jnp.einsum("qe,perfj->prfqj", cosines, imag_part, precision=high)
        - jnp.einsum("qe,perfj->prfqj", sines, real_part, precision=high)
    )
    power = 0.5 * jnp.sum(east_real * east_real + east_imag * east_imag, axis=0)
    return power.reshape(power.shape[0], power.shape[1], -1)


def dedisperse(spectrum, dm_delay, frames):
    base_cos, base_sin = phase_pair(jnp.transpose(dm_delay), frames)
    beams_dev = spectrum.shape[3]
    nfreq = spectrum.shape[2]

    def one_term(carry, block):
        cosine, sine = carry
        cos_half = cosine.astype(jnp.bfloat16)
        sin_half = sine.astype(jnp.bfloat16)
        upper = jnp.concatenate([cos_half, sin_half], axis=1)
        lower = jnp.concatenate([-sin_half, cos_half], axis=1)
        right = jnp.concatenate([upper, lower], axis=0)
        left = block.reshape(2 * nfreq, beams_dev)
        result = lax.dot_general(
            left, right, (((0,), (0,)), ((), ())), preferred_element_type=jnp.float32
        )
        next_cos = cosine * base_cos - sine * base_sin
        next_sin = sine * base_cos + cosine * base_sin
        return ((next_cos, next_sin), result)

    start = (jnp.ones(base_cos.shape, jnp.float32), jnp.zeros(base_cos.shape, jnp.float32))
    final, trials = lax.scan(one_term, start, spectrum)
    return trials.reshape(trials.shape[0], beams_dev, 2, -1)


def synthesis(trials, frames, nfreq):
    terms = frames // 2 + 1
    moment = lax.broadcasted_iota(jnp.int32, (frames, terms), 0)
    harmonic = lax.broadcasted_iota(jnp.int32, (frames, terms), 1)
    cosine, sine = phase_pair(moment * harmonic, frames)
    weight = jnp.where((harmonic == 0) | (harmonic * 2 == frames), 1.0, 2.0).astype(jnp.float32)
    weight = weight / (frames * math.sqrt(nfreq))
    table = jnp.stack([cosine * weight, -sine * weight], axis=1)
    return jnp.einsum("tuk,kbud->btd", table, trials, precision=lax.Precision.HIGHEST)


def body(raw, cell_feed, dm_delay):
    feed_dev, frames, samples = raw.shape
    nfreq = samples // 2
    table = channel_table(samples, nfreq)
    spectra = jnp.dot(
        raw.reshape(feed_dev * frames, samples), table, preferred_element_type=jnp.float32
    )
    spectra = spectra.astype(jnp.bfloat16).reshape(feed_dev, frames, 2, nfreq)
    cells = cell_feed.shape[0] // 4
    polar = lax.broadcasted_iota(jnp.int32, (2, 4, cells), 0)
    feed_index = 2 * cell_feed.reshape(1, 4, cells) + polar
    table_sky = sky_table(cells)
    arrived = lax.all_to_all(spectra, "wide", split_axis=3, concat_axis=0, tiled=True)
    power = beam_power(arrived, feed_index, table_sky)
    centred = (power - jnp.mean(power, axis=0, keepdims=True)).astype(jnp.bfloat16)
    time_table = transform_table(frames)
    local = jnp.einsum("okr,rfb->kofb", time_table, centred, preferred_element_type=jnp.float32)
    spectrum = lax.all_to_all(
        local.astype(jnp.bfloat16), "wide", split_axis=3, concat_axis=2, tiled=True
    )
    trials = dedisperse(spectrum, dm_delay, frames)
    return synthesis(trials, frames, nfreq)


def solution(mesh):
    placed = (P(("grp", "wide"), None, None), P(), P())
    return jax.shard_map(
        body, mesh=mesh, in_specs=placed, out_specs=P(("grp", "wide"), None, None), check_vma=False
    )
```

profile of v0, /device:TPU:13, one launch (start us, length us, event | category | flops | bytes accessed | tf_op | source)
XLA Modules:
  0.0 774.5 jit_solution(11408778004443474924)
XLA Ops:
  0.0 34.1 %multiply_convert_fusion = (bf16[2048,1024]{1,0:T(8,128)(2,1)S(1)}, bf16[2048,1024]{1,0:T(8,128)(2,1)S(1)}) fusion(), kind=kLoop, calls=%fused_computation.36 | loop fusion | flops 39845888 | bytes 8388608 | tf_op jit(solution)/shard_map/convert.3
  34.1 20.6 %convert_bitcast_fusion = bf16[2048,2048]{0,1:T(8,128)(2,1)} fusion(bf16[2048,2048]{1,0:T(8,128)(2,1)S(1)} %bitcast.101, bf16[2048,1024]{1,0:T(8,128)(2,1)S(1)} %get-tuple-element.115, bf16[2048,1024]{1,0:T(8,128)(2,1)S(1)} %get-tuple-element.116), kind=kOutput, calls=%fused_computation.35 | convolution fusion | flops 17200840704 | bytes 25165824 | tf_op jit(solution)/shard_map/dot_general | solution.py:104
  54.7 12.4 %copy.57 = bf16[2048,2048]{1,0:T(8,128)(2,1)} copy(bf16[2048,2048]{0,1:T(8,128)(2,1)} %convert_bitcast_fusion) | data formatting | bytes 16777216 | tf_op jit(solution)/shard_map/convert_element_type | solution.py:107
  67.1 14.5 %reshape.314 = bf16[128,16,2,1024]{3,2,1,0:T(2,128)(2,1)} reshape(bf16[2048,2048]{1,0:T(8,128)(2,1)} %copy.57) | data formatting | bytes 16777216 | tf_op jit(solution)/shard_map/reshape | solution.py:107
  81.6 16.8 %copy.58 = bf16[128,16,2,1024]{0,1,2,3:T(8,128)(2,1)} copy(bf16[128,16,2,1024]{3,2,1,0:T(2,128)(2,1)} %reshape.314) | data formatting | bytes 16777216 | tf_op jit(solution)/shard_map/reshape | solution.py:107
  98.4 7.0 all-to-all-start
  107.7 179.9 %all-to-all-done = bf16[128,16,2,1024]{0,1,2,3:T(8,128)(2,1)} async-done(((bf16[128,16,2,1024]{0,1,2,3:T(8,128)(2,1)}), bf16[128,16,2,1024]{0,1,2,3:T(8,128)(2,1)}, u32[]{:S(2)}, u32[]{:S(2)}) %all-to-all-start) | async-done | bytes 8388640 | tf_op jit(solution)/shard_map/all_to_all | solution.py:112
  287.6 29.0 %copy.82 = bf16[16,128,16,2,64]{4,2,3,1,0:T(8,128)(2,1)} copy(bf16[16,128,16,2,64]{1,2,3,4,0:T(8,128)(2,1)} %bitcast.5) | data formatting | bytes 16777216 | tf_op jit(solution)/shard_map/all_to_all | solution.py:112
  316.7 25.0 %gather_fusion = bf16[2048,16,2,64]{3,1,2,0:T(8,128)(2,1)} fusion(bf16[2048,16,2,64]{3,1,2,0:T(8,128)(2,1)} %bitcast.92, s32[2048]{0:T(1024)S(1)} %broadcast_clamp_fusion), kind=kCustom, calls=%fused_computation | custom fusion | bytes 16785408 | tf_op jit(solution)/shard_map/jit(_take)/gather | solution.py:44
  341.7 19.8 %copy.83 = bf16[2,4,256,16,2,64]{2,1,0,5,4,3:T(4,128)(2,1)} copy(bf16[2,4,256,16,2,64]{5,3,4,2,1,0:T(8,128)(2,1)} %bitcast.93) | data formatting | bytes 16777216 | tf_op jit(solution)/shard_map/jit(_take)/gather | solution.py:44
  361.4 5.8 select_bitcast_fusion
  367.2 8.2 %fusion.39 = f32[2,2,4,16,64,256]{5,4,1,3,2,0:T(8,128)} fusion(bf16[2,4,256,16,2,64,1]{2,1,0,5,4,3,6:T(4,128)(2,1)S(1)} %select_bitcast_fusion, f32[256,1,256,2]{2,0,3,1:T(8,128)S(1)} %get-tuple-element.112, f32[256,1,256,2]{2,0,3,1:T(8,128)S(1)} %get-tuple-element.111), kind=kOutput, calls=%fused_computation.49 | convolution fusion | flops 4295753728 | bytes 26214400 | tf_op jit(solution)/shard_map/joni,penrif->poerfj/dot_general | solution.py:46
  375.4 6.5 slice_bitcast_fusion.1
  382.0 18.8 %fusion.31 = f32[2,16,64,256,4]{3,4,2,1,0:T(4,128)} fusion(f32[4,4,1,1,1]{1,0,4,3,2:T(4,128)S(1)} %copy-done.3, f32[2,4,16,64,256]{4,3,2,1,0:T(8,128)S(1)} %get-tuple-element.108), kind=kOutput, calls=%fused_computation.41 | convolution fusion | flops 100663296 | bytes 16777280 | tf_op jit(solution)/shard_map/qe,perfj->prfqj/dot_general | solution.py:57
  400.8 18.4 %fusion.33 = f32[2,16,64,256,4]{3,4,2,1,0:T(4,128)} fusion(f32[4,4,1,1,1]{1,0,4,3,2:T(4,128)S(1)} %copy-done.4, f32[2,4,16,64,256]{4,3,2,1,0:T(8,128)S(1)} %get-tuple-element.108), kind=kOutput, calls=%fused_computation.43 | convolution fusion | flops 100663296 | bytes 16777280 | tf_op jit(solution)/shard_map/qe,perfj->prfqj/dot_general | solution.py:54
  419.2 18.5 %fusion.35 = f32[2,16,64,256,4]{3,4,2,1,0:T(4,128)} fusion(f32[4,4,1,1,1]{1,0,4,3,2:T(4,128)S(1)} %copy-done.4, f32[2,4,16,64,256]{4,3,2,1,0:T(8,128)S(1)} %get-tuple-element.107), kind=kOutput, calls=%fused_computation.45 | convolution fusion | flops 100663296 | bytes 16777280 | tf_op jit(solution)/shard_map/qe,perfj->prfqj/dot_general | solution.py:58
  437.7 32.8 %add_reduce_fusion = f32[16,64,256,4]{2,3,1,0:T(4,128)} fusion(f32[2,16,64,256,4]{3,4,2,1,0:T(4,128)} %fusion.31, f32[2,16,64,256,4]{3,4,2,1,0:T(4,128)} %fusion.35, f32[2,16,64,256,4]{3,4,2,1,0:T(4,128)} %fusion.33, f32[4,4,1,1,1]{1,0,4,3,2:T(4,128)S(1)} %copy-done.3, f32[2,4,16,64,256]{4,3,2,1,0:T(8,128)} %copy-done.1), kind=kOutput, calls=%fused_computation.33 | convolution fusion | flops 116391936 | bytes 37748800 | tf_op jit(solution)/shard_map/qe,perfj->prfqj/dot_general | solution.py:53
  470.5 5.4 multiply_bitcast_fusion
  476.9 5.8 mul.255
  482.8 7.1 convert_bitcast_fusion.1
  489.9 14.7 %copy.69 = bf16[9,2,64,1024]{2,1,0,3:T(2,128)(2,1)} copy(bf16[9,2,64,1024]{3,0,1,2:T(8,128)(2,1)} %convert_bitcast_fusion.1) | data formatting | bytes 4718592 | tf_op jit(solution)/shard_map/convert_element_type | solution.py:118
  504.6 7.8 %reshape.334 = bf16[16,2,36864]{2,1,0:T(2,128)(2,1)} reshape(bf16[1024,9,2,64]{3,2,1,0:T(2,128)(2,1)} %bitcast.94) | data formatting | bytes 4718592
  512.5 5.1 all-to-all-start.1
  517.6 5.3 copy.56
  523.0 18.4 %fusion.55 = (f32[1024,1024]{1,0:T(8,128)}, f32[1024,1024]{1,0:T(8,128)}) fusion(s32[1024,1024]{0,1:T(8,128)} %copy.56), kind=kLoop, calls=%fused_computation.65 | loop fusion | flops 13631488 | bytes 12582912 | tf_op jit(solution)/shard_map/sin | solution.py:14
  541.4 29.1 %all-to-all-done.1 = bf16[16,2,36864]{2,1,0:T(2,128)(2,1)S(1)} async-done(((bf16[16,2,36864]{2,1,0:T(2,128)(2,1)}), bf16[16,2,36864]{2,1,0:T(2,128)(2,1)S(1)}, u32[]{:S(2)}, u32[]{:S(2)}) %all-to-all-start.1) | async-done | bytes 2359328 | tf_op jit(solution)/shard_map/all_to_all | solution.py:117
  570.5 5.3 reshape.335
  575.8 11.5 %copy.90 = bf16[9,2,64,16,64]{4,2,3,1,0:T(8,128)(2,1)} copy(bf16[9,2,64,16,64]{2,1,0,4,3:T(2,128)(2,1)} %bitcast.95) | data formatting | bytes 4718592 | tf_op jit(solution)/shard_map/all_to_all | solution.py:117
  587.2 166.2 %while.15 = (s32[]{:T(128)}, f32[1024,1024]{1,0:T(8,128)}, f32[1024,1024]{1,0:T(8,128)}, f32[9,64,2048]{2,1,0:T(8,128)}, f32[1024,1024]{1,0:T(8,128)}, /*index=5...) while((s32[]{:T(128)}, f32[1024,1024]{1,0:T(8,128)}, ...), condition=%wide.region_3.4_spmd.clone, body=%wide.region_2.3_spmd.clone.sunk | while | flops 584056832 | bytes 64225924 | solution.py:85
  587.2 1.5 fusion.105
  588.7 1.1 constant_dynamic-slice_fusion.2
  589.8 2.4 fusion.106
  592.3 8.2 %multiply_add_fusion.2 = (f32[1024,1024]{1,0:T(8,128)}, f32[1024,1024]{1,0:T(8,128)}) fusion(f32[1024,1024]{1,0:T(8,128)S(1)} %copy-done, f32[1024,1024]{1,0:T(8,128)} %get-tuple-element.196, f32[1024,1024]{1,0:T(8,128)} %get-tuple-element.185, f32[1024,1024]{1,0:T(8,128)} %get-tuple-element.184, pred[]{:T(512)S(6)} %compare.38), kind=kLoop, calls=%fused_computation.9.clone.1 | loop fusion | flops 8388608 | bytes 25165824 | tf_op jit(solution)/shard_map/while/body/eval_jaxpr/add | solution.py:81
  600.4 4.9 fusion.105
  605.4 1.1 constant_dynamic-slice_fusion.2
  606.5 2.5 fusion.106
  608.9 10.6 %multiply_add_fusion.2 = (f32[1024,1024]{1,0:T(8,128)}, f32[1024,1024]{1,0:T(8,128)}) fusion(f32[1024,1024]{1,0:T(8,128)S(1)} %copy-done, f32[1024,1024]{1,0:T(8,128)} %get-tuple-element.196, f32[1024,1024]{1,0:T(8,128)} %get-tuple-element.185, f32[1024,1024]{1,0:T(8,128)} %get-tuple-element.184, pred[]{:T(512)S(6)} %compare.38), kind=kLoop, calls=%fused_computation.9.clone.1 | loop fusion | flops 8388608 | bytes 25165824 | tf_op jit(solution)/shard_map/while/body/eval_jaxpr/add | solution.py:81
  619.6 4.9 fusion.105
  624.5 1.1 constant_dynamic-slice_fusion.2
  625.6 2.4 fusion.106
  628.1 10.6 %multiply_add_fusion.2 = (f32[1024,1024]{1,0:T(8,128)}, f32[1024,1024]{1,0:T(8,128)}) fusion(f32[1024,1024]{1,0:T(8,128)S(1)} %copy-done, f32[1024,1024]{1,0:T(8,128)} %get-tuple-element.196, f32[1024,1024]{1,0:T(8,128)} %get-tuple-element.185, f32[1024,1024]{1,0:T(8,128)} %get-tuple-element.184, pred[]{:T(512)S(6)} %compare.38), kind=kLoop, calls=%fused_computation.9.clone.1 | loop fusion | flops 8388608 | bytes 25165824 | tf_op jit(solution)/shard_map/while/body/eval_jaxpr/add | solution.py:81
  638.7 4.9 fusion.105
  643.6 1.1 constant_dynamic-slice_fusion.2
  644.7 2.4 fusion.106
  647.2 10.6 %multiply_add_fusion.2 = (f32[1024,1024]{1,0:T(8,128)}, f32[1024,1024]{1,0:T(8,128)}) fusion(f32[1024,1024]{1,0:T(8,128)S(1)} %copy-done, f32[1024,1024]{1,0:T(8,128)} %get-tuple-element.196, f32[1024,1024]{1,0:T(8,128)} %get-tuple-element.185, f32[1024,1024]{1,0:T(8,128)} %get-tuple-element.184, pred[]{:T(512)S(6)} %compare.38), kind=kLoop, calls=%fused_computation.9.clone.1 | loop fusion | flops 8388608 | bytes 25165824 | tf_op jit(solution)/shard_map/while/body/eval_jaxpr/add | solution.py:81
  657.8 4.9 fusion.105
  662.8 1.1 constant_dynamic-slice_fusion.2
  663.9 2.4 fusion.106
  666.3 10.6 %multiply_add_fusion.2 = (f32[1024,1024]{1,0:T(8,128)}, f32[1024,1024]{1,0:T(8,128)}) fusion(f32[1024,1024]{1,0:T(8,128)S(1)} %copy-done, f32[1024,1024]{1,0:T(8,128)} %get-tuple-element.196, f32[1024,1024]{1,0:T(8,128)} %get-tuple-element.185, f32[1024,1024]{1,0:T(8,128)} %get-tuple-element.184, pred[]{:T(512)S(6)} %compare.38), kind=kLoop, calls=%fused_computation.9.clone.1 | loop fusion | flops 8388608 | bytes 25165824 | tf_op jit(solution)/shard_map/while/body/eval_jaxpr/add | solution.py:81
  676.9 4.9 fusion.105
  681.9 1.1 constant_dynamic-slice_fusion.2
  683.0 2.4 fusion.106
  685.4 10.6 %multiply_add_fusion.2 = (f32[1024,1024]{1,0:T(8,128)}, f32[1024,1024]{1,0:T(8,128)}) fusion(f32[1024,1024]{1,0:T(8,128)S(1)} %copy-done, f32[1024,1024]{1,0:T(8,128)} %get-tuple-element.196, f32[1024,1024]{1,0:T(8,128)} %get-tuple-element.185, f32[1024,1024]{1,0:T(8,128)} %get-tuple-element.184, pred[]{:T(512)S(6)} %compare.38), kind=kLoop, calls=%fused_computation.9.clone.1 | loop fusion | flops 8388608 | bytes 25165824 | tf_op jit(solution)/shard_map/while/body/eval_jaxpr/add | solution.py:81
  696.0 4.9 fusion.105
  702.1 2.5 fusion.106
  704.5 10.6 %multiply_add_fusion.2 = (f32[1024,1024]{1,0:T(8,128)}, f32[1024,1024]{1,0:T(8,128)}) fusion(f32[1024,1024]{1,0:T(8,128)S(1)} %copy-done, f32[1024,1024]{1,0:T(8,128)} %get-tuple-element.196, f32[1024,1024]{1,0:T(8,128)} %get-tuple-element.185, f32[1024,1024]{1,0:T(8,128)} %get-tuple-element.184, pred[]{:T(512)S(6)} %compare.38), kind=kLoop, calls=%fused_computation.9.clone.1 | loop fusion | flops 8388608 | bytes 25165824 | tf_op jit(solution)/shard_map/while/body/eval_jaxpr/add | solution.py:81
  715.2 4.9 fusion.105
  721.2 2.5 fusion.106
  723.7 10.6 %multiply_add_fusion.2 = (f32[1024,1024]{1,0:T(8,128)}, f32[1024,1024]{1,0:T(8,128)}) fusion(f32[1024,1024]{1,0:T(8,128)S(1)} %copy-done, f32[1024,1024]{1,0:T(8,128)} %get-tuple-element.196, f32[1024,1024]{1,0:T(8,128)} %get-tuple-element.185, f32[1024,1024]{1,0:T(8,128)} %get-tuple-element.184, pred[]{:T(512)S(6)} %compare.38), kind=kLoop, calls=%fused_computation.9.clone.1 | loop fusion | flops 8388608 | bytes 25165824 | tf_op jit(solution)/shard_map/while/body/eval_jaxpr/add | solution.py:81
  734.3 4.9 fusion.105
  740.4 2.4 fusion.106
  742.8 10.6 %multiply_add_fusion.2 = (f32[1024,1024]{1,0:T(8,128)}, f32[1024,1024]{1,0:T(8,128)}) fusion(f32[1024,1024]{1,0:T(8,128)S(1)} %copy-done, f32[1024,1024]{1,0:T(8,128)} %get-tuple-element.196, f32[1024,1024]{1,0:T(8,128)} %get-tuple-element.185, f32[1024,1024]{1,0:T(8,128)} %get-tuple-element.184, pred[]{:T(512)S(6)} %compare.38), kind=kLoop, calls=%fused_computation.9.clone.1 | loop fusion | flops 8388608 | bytes 25165824 | tf_op jit(solution)/shard_map/while/body/eval_jaxpr/add | solution.py:81
  753.5 7.4 reshape.315
  760.8 13.1 %fusion.48 = f32[64,16,1024]{2,1,0:T(8,128)} fusion(f32[9,64,2,1024]{3,2,1,0:T(2,128)} %reshape.315, f32[16,1,9]{2,0,1:T(8,128)S(1)} %get-tuple-element.114, f32[16,1,9]{2,0,1:T(8,128)S(1)} %get-tuple-element.113), kind=kOutput, calls=%fused_computation.60 | convolution fusion | flops 226492704 | bytes 8914048 | tf_op jit(solution)/shard_map/tuk,kbud->btd/dot_general | solution.py:97
  (52 shorter events, 6.7 us)
Async XLA Ops:
  0.0 34.1 %copy-start.6 = (bf16[128,16,2048]{2,1,0:T(8,128)(2,1)S(1)}, bf16[128,16,2048]{2,1,0:T(8,128)(2,1)}, u32[]{:S(2)}) copy-start(bf16[128,16,2048]{2,1,0:T(8,128)(2,1)} %param.7) | copy-start | bytes 25165828
  98.4 7.0 copy-start.5
  98.4 189.2 %all-to-all-start = ((bf16[128,16,2,1024]{0,1,2,3:T(8,128)(2,1)}), bf16[128,16,2,1024]{0,1,2,3:T(8,128)(2,1)}, u32[]{:S(2)}, u32[]{:S(2)}) async-start(bf16[128,16,2,1024]{0,1,2,3:T(8,128)(2,1)} %copy.58), calls=%async_computation | async-start | bytes 16777216 | tf_op jit(solution)/shard_map/all_to_all | solution.py:112
  375.4 6.5 copy-start.3
  381.9 37.2 %copy-start.1 = (f32[2,4,16,64,256]{4,3,2,1,0:T(8,128)}, f32[2,4,16,64,256]{4,3,2,1,0:T(8,128)S(1)}, u32[]{:S(2)}) copy-start(f32[2,4,16,64,256]{4,3,2,1,0:T(8,128)S(1)} %get-tuple-element.107) | copy-start | bytes 25165828
  382.0 18.8 %copy-start.4 = (f32[4,4,1,1,1]{1,0,4,3,2:T(4,128)S(1)}, f32[4,4,1,1,1]{1,0,4,3,2:T(4,128)}, u32[]{:S(2)}) copy-start(f32[4,4,1,1,1]{1,0,4,3,2:T(4,128)} %constant.123) | copy-start | bytes 196
  470.5 5.4 copy-start.2
  512.5 58.0 %all-to-all-start.1 = ((bf16[16,2,36864]{2,1,0:T(2,128)(2,1)}), bf16[16,2,36864]{2,1,0:T(2,128)(2,1)S(1)}, u32[]{:S(2)}, u32[]{:S(2)}) async-start(bf16[16,2,36864]{2,1,0:T(2,128)(2,1)} %reshape.334), calls=%async_computation.1 | async-start | bytes 4718592 | tf_op jit(solution)/shard_map/all_to_all | solution.py:117
  589.8 2.4 copy-start
  606.5 2.5 copy-start
  625.6 2.4 copy-start
  644.7 2.4 copy-start
  663.8 2.4 copy-start
  682.9 2.4 copy-start
  702.1 2.5 copy-start
  721.2 2.5 copy-start
  740.4 2.5 copy-start
where the time goes:
time: 784 us; the launch traced here: 774 us
  waiting for transfers between devices  209 us (27%)
  other arithmetic  201 us (26%)
  local copies, waits for them, and re-layouts  192 us (24%)
  matrix products  160 us (20%)
  starting transfers between devices  12.1 us (2%)
    all_to_all x1, waiting for transfers between devices, body(): lax.all_to_all(spectra, 'wide', split_axis=3, concat_axis=0, tiled=True)  180 us
    add x9, other arithmetic, one_term(): next_sin = sine * base_cos + cosine * base_sin  93.3 us
    gather x2, local copies, waits for them, and re-layouts, beam_power(): grid = jnp.take(spec, feed_index.reshape(-1), axis=0)  44.8 us
    neg x9, other arithmetic, one_term(): lower = jnp.concatenate([-sin_half, cos_half], axis=1)  41 us
    another operation x2, other arithmetic  34.1 us
    dot_general x1, matrix products, beam_power(): jnp.einsum('qe,perfj->prfqj', cosines, real_part, precision=high)  32.8 us
    reshape x2, local copies, waits for them, and re-layouts, body(): spectra = spectra.astype(jnp.bfloat16).reshape(feed_dev, frames, 2, nfreq)  31.3 us
    all_to_all x1, waiting for transfers between devices, body(): lax.all_to_all(local.astype(jnp.bfloat16), 'wide', split_axis=3, concat_a...  29.1 us
  transfers between devices with their start and end apart: 2, of which 2 were waited for; matrix products, arithmetic and copies ran while one was open for 3% of the time, Pallas kernels for 0%

commit v1 on v0

--- a/solution.py
+++ b/solution.py
@@ -7,6 +7,17 @@
 
 EAST_COSINE = np.array([[1, 1, 1, 1], [1, 0, -1, 0], [1, -1, 1, -1], [1, 0, -1, 0]], np.float32)
 EAST_SINE = np.array([[0, 0, 0, 0], [0, 1, 0, -1], [0, 0, 0, 0], [0, -1, 0, 1]], np.float32)
+
+
+def split_up(shard, dim, size):
+    before, after = (shard.shape[:dim], shard.shape[dim + 1 :])
+    return jnp.moveaxis(shard.reshape(*before, size, -1, *after), dim, 0)
+
+
+def in_order(blocks, dim):
+    blocks = jnp.moveaxis(blocks, 0, dim)
+    shape = blocks.shape
+    return blocks.reshape(*shape[:dim], shape[dim] * shape[dim + 1], *shape[dim + 2 :])
 
 
 def phase_pair(count, length):
@@ -114,9 +125,15 @@
     centred = (power - jnp.mean(power, axis=0, keepdims=True)).astype(jnp.bfloat16)
     time_table = transform_table(frames)
     local = jnp.einsum("okr,rfb->kofb", time_table, centred, preferred_element_type=jnp.float32)
-    spectrum = lax.all_to_all(
-        local.astype(jnp.bfloat16), "wide", split_axis=3, concat_axis=2, tiled=True
-    )
+    value = local.astype(jnp.bfloat16)
+    count_2, index = (lax.axis_size("wide"), lax.axis_index("wide"))
+    tiles = split_up(value, 3, count_2)
+    outs = [tiles[index]]
+    for step in range(1, count_2):
+        sent = tiles[(index + step) % count_2]
+        outs.append(lax.ppermute(sent, "wide", [(i, (i + step) % count_2) for i in range(count_2)]))
+    tiles = jnp.stack(outs)[(index - jnp.arange(count_2)) % count_2]
+    spectrum = in_order(tiles, 2)
     trials = dedisperse(spectrum, dm_delay, frames)
     return synthesis(trials, frames, nfreq)
 

time: 784 us -> 839 us (1.070)
  waiting for transfers between devices: 209 us -> 248 us
  local copies, waits for them, and re-layouts: 192 us -> 204 us
    ppermute x0 -> x15, waiting for transfers between devices: none -> 92.8 us  [body(): lax.ppermute(sent, 'wide', [(i, (i + step) % count_2) for i in range(coun...]
    all_to_all x1 -> x0, waiting for transfers between devices: 29.1 us -> none  [body(): lax.all_to_all(local.astype(jnp.bfloat16), 'wide', split_axis=3, concat_a...]
    all_to_all x1, waiting for transfers between devices: 180 us -> 155 us  [body(): lax.all_to_all(spectra, 'wide', split_axis=3, concat_axis=0, tiled=True)]
    another operation x0 -> x2, local copies, waits for them, and re-layouts: none -> 21.9 us
    convert_element_type x1, local copies, waits for them, and re-layouts: 14.7 us -> 1.43 us  [body(): value = local.astype(jnp.bfloat16)]
    all_to_all x1 -> x0, local copies, waits for them, and re-layouts: 11.5 us -> none  [body(): lax.all_to_all(local.astype(jnp.bfloat16), 'wide', split_axis=3, concat_a...]
    unnamed x16 -> x49, local copies, waits for them, and re-layouts: 18.5 us -> 23.3 us
  transfers between devices with their start and end apart: 2 -> 16, of which waited for: 2 -> 11; matrix products, arithmetic and copies ran while one was open for 3% -> 5% of each run, Pallas kernels for 0% -> 0%
where the time goes in v1:
time: 839 us; the launch traced here: 828 us
  waiting for transfers between devices  248 us (30%)
  local copies, waits for them, and re-layouts  204 us (24%)
  other arithmetic  202 us (24%)
  matrix products  157 us (19%)
  starting transfers between devices  15.6 us (2%)
    all_to_all x1, waiting for transfers between devices, body(): lax.all_to_all(spectra, 'wide', split_axis=3, concat_axis=0, tiled=True)  155 us
    add x9, other arithmetic, one_term(): next_sin = sine * base_cos + cosine * base_sin  93.3 us
    ppermute x15, waiting for transfers between devices, body(): lax.ppermute(sent, 'wide', [(i, (i + step) % count_2) for i in range(coun...  92.8 us
    gather x2, local copies, waits for them, and re-layouts, beam_power(): grid = jnp.take(spec, feed_index.reshape(-1), axis=0)  44.7 us
    neg x9, other arithmetic, one_term(): lower = jnp.concatenate([-sin_half, cos_half], axis=1)  41 us
    another operation x2, other arithmetic  34.1 us
    dot_general x1, matrix products, beam_power(): jnp.einsum('qe,perfj->prfqj', cosines, real_part, precision=high)  33 us
    reshape x2, local copies, waits for them, and re-layouts, body(): spectra = spectra.astype(jnp.bfloat16).reshape(feed_dev, frames, 2, nfreq)  31.4 us
  transfers between devices with their start and end apart: 16, of which 11 were waited for; matrix products, arithmetic and copies ran while one was open for 5% of the time, Pallas kernels for 0%

profile of v1, /device:TPU:13, one launch (start us, length us, event | category | flops | bytes accessed | tf_op | source)
XLA Modules:
  0.0 827.9 jit_solution(17816016748847486865)
XLA Ops:
  0.0 34.1 %multiply_convert_fusion = (bf16[2048,1024]{1,0:T(8,128)(2,1)S(1)}, bf16[2048,1024]{1,0:T(8,128)(2,1)S(1)}) fusion(), kind=kLoop, calls=%fused_computation.37 | loop fusion | flops 39845888 | bytes 8388608 | tf_op jit(solution)/shard_map/convert.3
  34.1 20.6 %convert_bitcast_fusion = bf16[2048,2048]{0,1:T(8,128)(2,1)} fusion(bf16[2048,2048]{1,0:T(8,128)(2,1)S(1)} %bitcast.190, bf16[2048,1024]{1,0:T(8,128)(2,1)S(1)} %get-tuple-element.131, bf16[2048,1024]{1,0:T(8,128)(2,1)S(1)} %get-tuple-element.132), kind=kOutput, calls=%fused_computation.36 | convolution fusion | flops 17200840704 | bytes 25165824 | tf_op jit(solution)/shard_map/dot_general | solution.py:115
  54.7 12.3 %copy.55 = bf16[2048,2048]{1,0:T(8,128)(2,1)} copy(bf16[2048,2048]{0,1:T(8,128)(2,1)} %convert_bitcast_fusion) | data formatting | bytes 16777216 | tf_op jit(solution)/shard_map/convert_element_type | solution.py:118
  67.0 14.5 %reshape.400 = bf16[128,16,2,1024]{3,2,1,0:T(2,128)(2,1)} reshape(bf16[2048,2048]{1,0:T(8,128)(2,1)} %copy.55) | data formatting | bytes 16777216 | tf_op jit(solution)/shard_map/reshape | solution.py:118
  81.6 16.9 %copy.56 = bf16[128,16,2,1024]{0,1,2,3:T(8,128)(2,1)} copy(bf16[128,16,2,1024]{3,2,1,0:T(2,128)(2,1)} %reshape.400) | data formatting | bytes 16777216 | tf_op jit(solution)/shard_map/reshape | solution.py:118
  98.4 7.3 all-to-all-start
  106.0 5.3 copy.54
  114.3 18.4 %fusion.55 = (f32[1024,1024]{1,0:T(8,128)}, f32[1024,1024]{1,0:T(8,128)}) fusion(s32[1024,1024]{0,1:T(8,128)} %copy.54), kind=kLoop, calls=%fused_computation.66 | loop fusion | flops 13631488 | bytes 12582912 | tf_op jit(solution)/shard_map/sin | solution.py:25
  132.7 155.2 %all-to-all-done = bf16[128,16,2,1024]{0,1,2,3:T(8,128)(2,1)} async-done(((bf16[128,16,2,1024]{0,1,2,3:T(8,128)(2,1)}), bf16[128,16,2,1024]{0,1,2,3:T(8,128)(2,1)}, u32[]{:S(2)}, u32[]{:S(2)}) %all-to-all-start) | async-done | bytes 8388640 | tf_op jit(solution)/shard_map/all_to_all | solution.py:123
  287.9 29.1 %copy.79 = bf16[16,128,16,2,64]{4,2,3,1,0:T(8,128)(2,1)} copy(bf16[16,128,16,2,64]{1,2,3,4,0:T(8,128)(2,1)} %bitcast.5) | data formatting | bytes 16777216 | tf_op jit(solution)/shard_map/all_to_all | solution.py:123
  317.0 25.0 %gather_fusion = bf16[2048,16,2,64]{3,1,2,0:T(8,128)(2,1)} fusion(bf16[2048,16,2,64]{3,1,2,0:T(8,128)(2,1)} %bitcast.167, s32[2048]{0:T(1024)S(1)} %broadcast_clamp_fusion), kind=kCustom, calls=%fused_computation | custom fusion | bytes 16785408 | tf_op jit(solution)/shard_map/jit(_take)/gather | solution.py:55
  342.0 19.7 %copy.80 = bf16[2,4,256,16,2,64]{2,1,0,5,4,3:T(4,128)(2,1)} copy(bf16[2,4,256,16,2,64]{5,3,4,2,1,0:T(8,128)(2,1)} %bitcast.168) | data formatting | bytes 16777216 | tf_op jit(solution)/shard_map/jit(_take)/gather | solution.py:55
  361.7 5.8 select_bitcast_fusion
  367.5 8.2 fusion.39
  375.7 6.5 slice_bitcast_fusion.1
  382.2 18.6 %fusion.31 = f32[2,16,64,256,4]{3,4,2,1,0:T(4,128)} fusion(f32[4,4,1,1,1]{1,0,4,3,2:T(4,128)S(1)} %copy-done.5, f32[2,4,16,64,256]{4,3,2,1,0:T(8,128)S(1)} %get-tuple-element.108), kind=kOutput, calls=%fused_computation.42 | convolution fusion | flops 100663296 | bytes 16777280 | tf_op jit(solution)/shard_map/qe,perfj->prfqj/dot_general | solution.py:68
  400.8 18.4 %fusion.33 = f32[2,16,64,256,4]{3,4,2,1,0:T(4,128)} fusion(f32[4,4,1,1,1]{1,0,4,3,2:T(4,128)S(1)} %copy-done.6, f32[2,4,16,64,256]{4,3,2,1,0:T(8,128)S(1)} %get-tuple-element.108), kind=kOutput, calls=%fused_computation.44 | convolution fusion | flops 100663296 | bytes 16777280 | tf_op jit(solution)/shard_map/qe,perfj->prfqj/dot_general | solution.py:65
  419.2 18.5 %fusion.35 = f32[2,16,64,256,4]{3,4,2,1,0:T(4,128)} fusion(f32[4,4,1,1,1]{1,0,4,3,2:T(4,128)S(1)} %copy-done.6, f32[2,4,16,64,256]{4,3,2,1,0:T(8,128)S(1)} %get-tuple-element.107), kind=kOutput, calls=%fused_computation.46 | convolution fusion | flops 100663296 | bytes 16777280 | tf_op jit(solution)/shard_map/qe,perfj->prfqj/dot_general | solution.py:69
  437.8 33.0 %add_reduce_fusion = f32[16,64,256,4]{2,3,1,0:T(4,128)} fusion(f32[2,16,64,256,4]{3,4,2,1,0:T(4,128)} %fusion.31, f32[2,16,64,256,4]{3,4,2,1,0:T(4,128)} %fusion.35, f32[2,16,64,256,4]{3,4,2,1,0:T(4,128)} %fusion.33, f32[4,4,1,1,1]{1,0,4,3,2:T(4,128)S(1)} %copy-done.5, f32[2,4,16,64,256]{4,3,2,1,0:T(8,128)} %copy-done.1), kind=kOutput, calls=%fused_computation.34 | convolution fusion | flops 116391936 | bytes 37748800 | tf_op jit(solution)/shard_map/qe,perfj->prfqj/dot_general | solution.py:64
  470.7 5.5 multiply_bitcast_fusion
  477.1 5.8 mul.255
  483.1 5.1 convert_bitcast_fusion.1
  489.6 4.7 reshape.401
  494.3 21.1 %constant_dynamic-slice_fusion.1 = (bf16[9,2,64,1,64]{4,3,2,1,0:T(2,128)(2,1)S(1)}, bf16[9,2,64,1,64]{4,3,2,1,0:T(2,128)(2,1)S(1)}, bf16[9,2,64,1,64]{4,3,2,1,0:...) fusion(bf16[9,2,64,16,64]{4,3,2,1,0:T(8,128)(2,1)} %reshape.401, ...), kind=kLoop, calls=%fused_computation.150 | loop fusion | bytes 4718656 | tf_op jit(solution)/shard_map/dynamic-slice.15
  518.5 4.0 collective-permute-start.4
  525.6 4.2 collective-permute-done.1
  530.6 5.4 collective-permute-done.2
  536.8 34.0 %collective-permute-done.3 = bf16[9,2,64,64]{3,2,1,0:T(8,128)(2,1)S(1)} collective-permute-done((bf16[9,2,64,64]{3,2,1,0:T(8,128)(2,1)S(1)}, bf16[9,2,64,64]{3,2,1,0:T(8,128)(2,1)S(1)}, u32[]{:S(2)}, u32[]{:S(2)}) %collective-permute-start.3) | collective-permute-done | bytes 147488 | tf_op jit(solution)/shard_map/ppermute | solution.py:134
  571.5 15.1 %collective-permute-done.4 = bf16[9,2,64,64]{3,2,1,0:T(8,128)(2,1)S(1)} collective-permute-done((bf16[9,2,64,64]{3,2,1,0:T(8,128)(2,1)S(1)}, bf16[9,2,64,64]{3,2,1,0:T(8,128)(2,1)S(1)}, u32[]{:S(2)}, u32[]{:S(2)}) %collective-permute-start.4) | collective-permute-done | bytes 147488 | tf_op jit(solution)/shard_map/ppermute | solution.py:134
  587.3 5.6 collective-permute-done.5
  593.8 11.7 %collective-permute-done.6 = bf16[9,2,64,64]{3,2,1,0:T(8,128)(2,1)S(1)} collective-permute-done((bf16[9,2,64,64]{3,2,1,0:T(8,128)(2,1)S(1)}, bf16[9,2,64,64]{3,2,1,0:T(8,128)(2,1)S(1)}, u32[]{:S(2)}, u32[]{:S(2)}) %collective-permute-start.6) | collective-permute-done | bytes 147488 | tf_op jit(solution)/shard_map/ppermute | solution.py:134
  606.3 8.7 %collective-permute-done.7 = bf16[9,2,64,64]{3,2,1,0:T(8,128)(2,1)S(1)} collective-permute-done((bf16[9,2,64,64]{3,2,1,0:T(8,128)(2,1)S(1)}, bf16[9,2,64,64]{3,2,1,0:T(8,128)(2,1)S(1)}, u32[]{:S(2)}, u32[]{:S(2)}) %collective-permute-start.7) | collective-permute-done | bytes 147488 | tf_op jit(solution)/shard_map/ppermute | solution.py:134
  622.2 4.7 collective-permute-done.13
  629.3 5.7 gather_fusion.1
  635.0 6.1 copy.83
  641.1 166.3 %while.15 = (s32[]{:T(128)}, f32[1024,1024]{1,0:T(8,128)}, f32[1024,1024]{1,0:T(8,128)}, f32[9,64,2048]{2,1,0:T(8,128)}, f32[1024,1024]{1,0:T(8,128)}, /*index=5...) while((s32[]{:T(128)}, f32[1024,1024]{1,0:T(8,128)}, ...), condition=%wide.region_3.4_spmd.clone, body=%wide.region_2.3_spmd.clone.sunk | while | flops 584056832 | bytes 64225924 | solution.py:96
  643.9 2.4 fusion.108
  646.3 8.2 multiply_add_fusion.2
  654.5 4.9 fusion.107
  660.5 2.4 fusion.108
  663.0 10.6 %multiply_add_fusion.2 = (f32[1024,1024]{1,0:T(8,128)}, f32[1024,1024]{1,0:T(8,128)}) fusion(f32[1024,1024]{1,0:T(8,128)S(1)} %copy-done, f32[1024,1024]{1,0:T(8,128)} %get-tuple-element.212, f32[1024,1024]{1,0:T(8,128)} %get-tuple-element.201, f32[1024,1024]{1,0:T(8,128)} %get-tuple-element.200, pred[]{:T(512)S(6)} %compare.60), kind=kLoop, calls=%fused_computation.10.clone.1 | loop fusion | flops 8388608 | bytes 25165824 | tf_op jit(solution)/shard_map/while/body/eval_jaxpr/add | solution.py:92
  673.6 4.9 fusion.107
  679.6 2.4 fusion.108
  682.1 10.6 %multiply_add_fusion.2 = (f32[1024,1024]{1,0:T(8,128)}, f32[1024,1024]{1,0:T(8,128)}) fusion(f32[1024,1024]{1,0:T(8,128)S(1)} %copy-done, f32[1024,1024]{1,0:T(8,128)} %get-tuple-element.212, f32[1024,1024]{1,0:T(8,128)} %get-tuple-element.201, f32[1024,1024]{1,0:T(8,128)} %get-tuple-element.200, pred[]{:T(512)S(6)} %compare.60), kind=kLoop, calls=%fused_computation.10.clone.1 | loop fusion | flops 8388608 | bytes 25165824 | tf_op jit(solution)/shard_map/while/body/eval_jaxpr/add | solution.py:92
  692.7 4.9 fusion.107
  698.7 2.4 fusion.108
  701.2 10.6 %multiply_add_fusion.2 = (f32[1024,1024]{1,0:T(8,128)}, f32[1024,1024]{1,0:T(8,128)}) fusion(f32[1024,1024]{1,0:T(8,128)S(1)} %copy-done, f32[1024,1024]{1,0:T(8,128)} %get-tuple-element.212, f32[1024,1024]{1,0:T(8,128)} %get-tuple-element.201, f32[1024,1024]{1,0:T(8,128)} %get-tuple-element.200, pred[]{:T(512)S(6)} %compare.60), kind=kLoop, calls=%fused_computation.10.clone.1 | loop fusion | flops 8388608 | bytes 25165824 | tf_op jit(solution)/shard_map/while/body/eval_jaxpr/add | solution.py:92
  711.8 4.9 fusion.107
  717.9 2.4 fusion.108
  720.3 10.6 %multiply_add_fusion.2 = (f32[1024,1024]{1,0:T(8,128)}, f32[1024,1024]{1,0:T(8,128)}) fusion(f32[1024,1024]{1,0:T(8,128)S(1)} %copy-done, f32[1024,1024]{1,0:T(8,128)} %get-tuple-element.212, f32[1024,1024]{1,0:T(8,128)} %get-tuple-element.201, f32[1024,1024]{1,0:T(8,128)} %get-tuple-element.200, pred[]{:T(512)S(6)} %compare.60), kind=kLoop, calls=%fused_computation.10.clone.1 | loop fusion | flops 8388608 | bytes 25165824 | tf_op jit(solution)/shard_map/while/body/eval_jaxpr/add | solution.py:92
  730.9 4.9 fusion.107
  737.0 2.4 fusion.108
  739.4 10.6 %multiply_add_fusion.2 = (f32[1024,1024]{1,0:T(8,128)}, f32[1024,1024]{1,0:T(8,128)}) fusion(f32[1024,1024]{1,0:T(8,128)S(1)} %copy-done, f32[1024,1024]{1,0:T(8,128)} %get-tuple-element.212, f32[1024,1024]{1,0:T(8,128)} %get-tuple-element.201, f32[1024,1024]{1,0:T(8,128)} %get-tuple-element.200, pred[]{:T(512)S(6)} %compare.60), kind=kLoop, calls=%fused_computation.10.clone.1 | loop fusion | flops 8388608 | bytes 25165824 | tf_op jit(solution)/shard_map/while/body/eval_jaxpr/add | solution.py:92
  750.0 4.9 fusion.107
  756.1 2.4 fusion.108
  758.5 10.6 %multiply_add_fusion.2 = (f32[1024,1024]{1,0:T(8,128)}, f32[1024,1024]{1,0:T(8,128)}) fusion(f32[1024,1024]{1,0:T(8,128)S(1)} %copy-done, f32[1024,1024]{1,0:T(8,128)} %get-tuple-element.212, f32[1024,1024]{1,0:T(8,128)} %get-tuple-element.201, f32[1024,1024]{1,0:T(8,128)} %get-tuple-element.200, pred[]{:T(512)S(6)} %compare.60), kind=kLoop, calls=%fused_computation.10.clone.1 | loop fusion | flops 8388608 | bytes 25165824 | tf_op jit(solution)/shard_map/while/body/eval_jaxpr/add | solution.py:92
  769.2 4.9 fusion.107
  775.2 2.4 fusion.108
  777.6 10.6 %multiply_add_fusion.2 = (f32[1024,1024]{1,0:T(8,128)}, f32[1024,1024]{1,0:T(8,128)}) fusion(f32[1024,1024]{1,0:T(8,128)S(1)} %copy-done, f32[1024,1024]{1,0:T(8,128)} %get-tuple-element.212, f32[1024,1024]{1,0:T(8,128)} %get-tuple-element.201, f32[1024,1024]{1,0:T(8,128)} %get-tuple-element.200, pred[]{:T(512)S(6)} %compare.60), kind=kLoop, calls=%fused_computation.10.clone.1 | loop fusion | flops 8388608 | bytes 25165824 | tf_op jit(solution)/shard_map/while/body/eval_jaxpr/add | solution.py:92
  788.3 4.9 fusion.107
  794.3 2.4 fusion.108
  796.8 10.6 %multiply_add_fusion.2 = (f32[1024,1024]{1,0:T(8,128)}, f32[1024,1024]{1,0:T(8,128)}) fusion(f32[1024,1024]{1,0:T(8,128)S(1)} %copy-done, f32[1024,1024]{1,0:T(8,128)} %get-tuple-element.212, f32[1024,1024]{1,0:T(8,128)} %get-tuple-element.201, f32[1024,1024]{1,0:T(8,128)} %get-tuple-element.200, pred[]{:T(512)S(6)} %compare.60), kind=kLoop, calls=%fused_computation.10.clone.1 | loop fusion | flops 8388608 | bytes 25165824 | tf_op jit(solution)/shard_map/while/body/eval_jaxpr/add | solution.py:92
  807.4 7.4 reshape.403
  814.8 12.9 %fusion.48 = f32[64,16,1024]{2,1,0:T(8,128)} fusion(f32[9,64,2,1024]{3,2,1,0:T(2,128)} %reshape.403, f32[16,1,9]{2,0,1:T(8,128)S(1)} %copy-done.4, f32[16,1,9]{2,0,1:T(8,128)S(1)} %copy-done.3), kind=kOutput, calls=%fused_computation.61 | convolution fusion | flops 226492704 | bytes 8914048 | tf_op jit(solution)/shard_map/tuk,kbud->btd/dot_general | solution.py:108
  (118 shorter events, 37.0 us)
Async XLA Ops:
  0.0 34.1 %copy-start.8 = (bf16[128,16,2048]{2,1,0:T(8,128)(2,1)S(1)}, bf16[128,16,2048]{2,1,0:T(8,128)(2,1)}, u32[]{:S(2)}) copy-start(bf16[128,16,2048]{2,1,0:T(8,128)(2,1)} %param.7) | copy-start | bytes 25165828
  98.4 7.5 copy-start.7
  98.4 189.5 %all-to-all-start = ((bf16[128,16,2,1024]{0,1,2,3:T(8,128)(2,1)}), bf16[128,16,2,1024]{0,1,2,3:T(8,128)(2,1)}, u32[]{:S(2)}, u32[]{:S(2)}) async-start(bf16[128,16,2,1024]{0,1,2,3:T(8,128)(2,1)} %copy.56), calls=%async_computation | async-start | bytes 16777216 | tf_op jit(solution)/shard_map/all_to_all | solution.py:123
  375.6 6.5 copy-start.5
  382.2 37.1 %copy-start.1 = (f32[2,4,16,64,256]{4,3,2,1,0:T(8,128)}, f32[2,4,16,64,256]{4,3,2,1,0:T(8,128)S(1)}, u32[]{:S(2)}) copy-start(f32[2,4,16,64,256]{4,3,2,1,0:T(8,128)S(1)} %get-tuple-element.107) | copy-start | bytes 25165828
  382.2 18.6 %copy-start.6 = (f32[4,4,1,1,1]{1,0,4,3,2:T(4,128)S(1)}, f32[4,4,1,1,1]{1,0,4,3,2:T(4,128)}, u32[]{:S(2)}) copy-start(f32[4,4,1,1,1]{1,0,4,3,2:T(4,128)} %constant.227) | copy-start | bytes 196
  470.7 5.5 copy-start.2
  515.5 8.3 collective-permute-start
  517.3 12.5 %collective-permute-start.1 = (bf16[9,2,64,64]{3,2,1,0:T(8,128)(2,1)S(1)}, bf16[9,2,64,64]{3,2,1,0:T(8,128)(2,1)S(1)}, u32[]{:S(2)}, u32[]{:S(2)}) collective-permute-start(bf16[9,2,64,64]{3,2,1,0:T(8,128)(2,1)S(1)} %bitcast.187), channel_id=1, source_target_pairs={{0,2},{1,3},{2,4},{3,5},{4,6},{5,7},{6,8},{7,9},{8,10},{9,11},{10,... | collective-permute-start | bytes 442376 | tf_op jit(solution)/shard_map/ppermute | solution.py:134
  517.4 18.6 %collective-permute-start.2 = (bf16[9,2,64,64]{3,2,1,0:T(8,128)(2,1)S(1)}, bf16[9,2,64,64]{3,2,1,0:T(8,128)(2,1)S(1)}, u32[]{:S(2)}, u32[]{:S(2)}) collective-permute-start(bf16[9,2,64,64]{3,2,1,0:T(8,128)(2,1)S(1)} %bitcast.186), channel_id=1, source_target_pairs={{0,3},{1,4},{2,5},{3,6},{4,7},{5,8},{6,9},{7,10},{8,11},{9,12},{10... | collective-permute-start | bytes 442376 | tf_op jit(solution)/shard_map/ppermute | solution.py:134
  517.5 53.2 %collective-permute-start.3 = (bf16[9,2,64,64]{3,2,1,0:T(8,128)(2,1)S(1)}, bf16[9,2,64,64]{3,2,1,0:T(8,128)(2,1)S(1)}, u32[]{:S(2)}, u32[]{:S(2)}) collective-permute-start(bf16[9,2,64,64]{3,2,1,0:T(8,128)(2,1)S(1)} %bitcast.185), channel_id=1, source_target_pairs={{0,4},{1,5},{2,6},{3,7},{4,8},{5,9},{6,10},{7,11},{8,12},{9,13},{1... | collective-permute-start | bytes 442376 | tf_op jit(solution)/shard_map/ppermute | solution.py:134
  518.5 68.1 %collective-permute-start.4 = (bf16[9,2,64,64]{3,2,1,0:T(8,128)(2,1)S(1)}, bf16[9,2,64,64]{3,2,1,0:T(8,128)(2,1)S(1)}, u32[]{:S(2)}, u32[]{:S(2)}) collective-permute-start(bf16[9,2,64,64]{3,2,1,0:T(8,128)(2,1)S(1)} %bitcast.184), channel_id=1, source_target_pairs={{0,5},{1,6},{2,7},{3,8},{4,9},{5,10},{6,11},{7,12},{8,13},{9,14},{... | collective-permute-start | bytes 442376 | tf_op jit(solution)/shard_map/ppermute | solution.py:134
  523.8 69.1 %collective-permute-start.5 = (bf16[9,2,64,64]{3,2,1,0:T(8,128)(2,1)S(1)}, bf16[9,2,64,64]{3,2,1,0:T(8,128)(2,1)S(1)}, u32[]{:S(2)}, u32[]{:S(2)}) collective-permute-start(bf16[9,2,64,64]{3,2,1,0:T(8,128)(2,1)S(1)} %bitcast.183), channel_id=1, source_target_pairs={{0,6},{1,7},{2,8},{3,9},{4,10},{5,11},{6,12},{7,13},{8,14},{9,15},... | collective-permute-start | bytes 442376 | tf_op jit(solution)/shard_map/ppermute | solution.py:134
  529.8 75.7 %collective-permute-start.6 = (bf16[9,2,64,64]{3,2,1,0:T(8,128)(2,1)S(1)}, bf16[9,2,64,64]{3,2,1,0:T(8,128)(2,1)S(1)}, u32[]{:S(2)}, u32[]{:S(2)}) collective-permute-start(bf16[9,2,64,64]{3,2,1,0:T(8,128)(2,1)S(1)} %bitcast.182), channel_id=1, source_target_pairs={{0,7},{1,8},{2,9},{3,10},{4,11},{5,12},{6,13},{7,14},{8,15},{9,0},... | collective-permute-start | bytes 442376 | tf_op jit(solution)/shard_map/ppermute | solution.py:134
  536.0 79.0 %collective-permute-start.7 = (bf16[9,2,64,64]{3,2,1,0:T(8,128)(2,1)S(1)}, bf16[9,2,64,64]{3,2,1,0:T(8,128)(2,1)S(1)}, u32[]{:S(2)}, u32[]{:S(2)}) collective-permute-start(bf16[9,2,64,64]{3,2,1,0:T(8,128)(2,1)S(1)} %bitcast.181), channel_id=1, source_target_pairs={{0,8},{1,9},{2,10},{3,11},{4,12},{5,13},{6,14},{7,15},{8,0},{9,1},... | collective-permute-start | bytes 442376 | tf_op jit(solution)/shard_map/ppermute | solution.py:134
  570.8 45.0 %collective-permute-start.8 = (bf16[9,2,64,64]{3,2,1,0:T(8,128)(2,1)S(1)}, bf16[9,2,64,64]{3,2,1,0:T(8,128)(2,1)S(1)}, u32[]{:S(2)}, u32[]{:S(2)}) collective-permute-start(bf16[9,2,64,64]{3,2,1,0:T(8,128)(2,1)S(1)} %bitcast.180), channel_id=1, source_target_pairs={{0,9},{1,10},{2,11},{3,12},{4,13},{5,14},{6,15},{7,0},{8,1},{9,2},... | collective-permute-start | bytes 442376 | tf_op jit(solution)/shard_map/ppermute | solution.py:134
  586.6 30.0 %collective-permute-start.9 = (bf16[9,2,64,64]{3,2,1,0:T(8,128)(2,1)S(1)}, bf16[9,2,64,64]{3,2,1,0:T(8,128)(2,1)S(1)}, u32[]{:S(2)}, u32[]{:S(2)}) collective-permute-start(bf16[9,2,64,64]{3,2,1,0:T(8,128)(2,1)S(1)} %bitcast.179), channel_id=1, source_target_pairs={{0,10},{1,11},{2,12},{3,13},{4,14},{5,15},{6,0},{7,1},{8,2},{9,3},... | collective-permute-start | bytes 442376 | tf_op jit(solution)/shard_map/ppermute | solution.py:134
  592.9 24.7 %collective-permute-start.10 = (bf16[9,2,64,64]{3,2,1,0:T(8,128)(2,1)S(1)}, bf16[9,2,64,64]{3,2,1,0:T(8,128)(2,1)S(1)}, u32[]{:S(2)}, u32[]{:S(2)}) collective-permute-start(bf16[9,2,64,64]{3,2,1,0:T(8,128)(2,1)S(1)} %bitcast.178), channel_id=1, source_target_pairs={{0,11},{1,12},{2,13},{3,14},{4,15},{5,0},{6,1},{7,2},{8,3},{9,4},{... | collective-permute-start | bytes 442376 | tf_op jit(solution)/shard_map/ppermute | solution.py:134
  605.5 12.8 %collective-permute-start.11 = (bf16[9,2,64,64]{3,2,1,0:T(8,128)(2,1)S(1)}, bf16[9,2,64,64]{3,2,1,0:T(8,128)(2,1)S(1)}, u32[]{:S(2)}, u32[]{:S(2)}) collective-permute-start(bf16[9,2,64,64]{3,2,1,0:T(8,128)(2,1)S(1)} %bitcast.177), channel_id=1, source_target_pairs={{0,12},{1,13},{2,14},{3,15},{4,0},{5,1},{6,2},{7,3},{8,4},{9,5},{1... | collective-permute-start | bytes 442376 | tf_op jit(solution)/shard_map/ppermute | solution.py:134
  615.0 6.4 collective-permute-start.12
  615.8 11.1 %collective-permute-start.13 = (bf16[9,2,64,64]{3,2,1,0:T(8,128)(2,1)S(1)}, bf16[9,2,64,64]{3,2,1,0:T(8,128)(2,1)S(1)}, u32[]{:S(2)}, u32[]{:S(2)}) collective-permute-start(bf16[9,2,64,64]{3,2,1,0:T(8,128)(2,1)S(1)} %bitcast.175), channel_id=1, source_target_pairs={{0,14},{1,15},{2,0},{3,1},{4,2},{5,3},{6,4},{7,5},{8,6},{9,7},{10,... | collective-permute-start | bytes 442376 | tf_op jit(solution)/shard_map/ppermute | solution.py:134
  616.5 12.0 %collective-permute-start.14 = (bf16[9,2,64,64]{3,2,1,0:T(8,128)(2,1)S(1)}, bf16[9,2,64,64]{3,2,1,0:T(8,128)(2,1)S(1)}, u32[]{:S(2)}, u32[]{:S(2)}) collective-permute-start(bf16[9,2,64,64]{3,2,1,0:T(8,128)(2,1)S(1)} %bitcast.174), channel_id=1, source_target_pairs={{0,15},{1,0},{2,1},{3,2},{4,3},{5,4},{6,5},{7,6},{8,7},{9,8},{10,9... | collective-permute-start | bytes 442376 | tf_op jit(solution)/shard_map/ppermute | solution.py:134
  643.9 2.4 copy-start
  660.5 2.4 copy-start
  679.6 2.4 copy-start
  698.7 2.5 copy-start
  717.9 2.4 copy-start
  737.0 2.4 copy-start
  756.1 2.5 copy-start
  775.2 2.4 copy-start
  794.3 2.4 copy-start
  807.4 7.4 copy-start.3
  807.4 7.4 copy-start.4
